TPU v7x, 32 devices: a whole 2x2x4 slice. The times are simulated.
32 devices in a mesh: expert: 4 (over x, core), ctx: 2 (over y), tensor: 4 (over z).
Axes of the slice: x: 2, y: 2, z: 4, core: 2. Of those that a mesh axis runs over, the one named last changes fastest.
Arguments:
- tokens: bfloat16 [64, 6144], P('expert', 'tensor'), may hold values from -6 to 6
- expert_ids: int32 [64, 2], P('expert'), may hold values from 0 to 3, all different within a row; in each aligned block of 8 rows (0 to 7, 8 to 15, ...) at most 4 rows name the same one
- route_gates: float32 [64, 2], P('expert'), may hold values from 0.2 to 1
- up_weight: bfloat16 [4, 12288, 6144], P('expert', 'ctx', 'tensor'), may hold values from -0.078125 to 0.078125
- down_weight: bfloat16 [4, 12288, 6144], P('expert', 'ctx', 'tensor'), may hold values from -0.0546875 to 0.0546875
Outputs:
- mixed: bfloat16 [64, 6144], P(('expert', 'ctx'), 'tensor')
Inputs may be any that keep to these rules, and one draw needn't show every extreme that they name: `expert_ids`: each token names 2 different experts. In each aligned block of 8 tokens at most 4 choices name one expert, and in some block one expert is named exactly 4 times. Every expert is named somewhere.
All inputs are finite; a program needn't handle non-finite values.
Results may differ from a plain program's by a relative error of at most 0.0057.
Values may be sent and summed in bfloat16 or wider, within the bound.
No kernel may reach another device: no remote copies, remote signals or barrier semaphores. Data moves between devices by JAX's collectives and lax.ppermute only.
A program may use at most 64 MiB of HBM per device.

v0:
```python
import jax
import jax.numpy as jnp
from jax import lax
from jax.sharding import PartitionSpec as P


def choice_slots(expert_ids, block_len, expert_count):
    top_count = expert_ids.shape[1]
    per_block = expert_ids.reshape(-1, block_len * top_count)
    marked = (
        per_block[:, :, None] == jnp.arange(expert_count, dtype=jnp.int32)[None, None, :]
    ).astype(jnp.int32)
    earlier = jnp.cumsum(marked, axis=1) - marked
    return jnp.sum(earlier * marked, axis=2).reshape(-1, top_count)


def local(tokens, expert_ids, route_gates, up_weight, down_weight):
    ctx_count = lax.axis_size("ctx")
    expert_count = lax.axis_size("expert")
    group_len = tokens.shape[0]
    width_local = tokens.shape[1]
    block_len = group_len // ctx_count
    capacity = block_len // 2
    per_expert = ctx_count * capacity
    ctx_index = lax.axis_index("ctx")
    slot_ids = choice_slots(expert_ids, block_len, expert_count)
    block_of = (jnp.arange(group_len, dtype=jnp.int32) // block_len)[:, None]
    dest_index = expert_ids * per_expert + block_of * capacity + slot_ids
    slot_range = jnp.arange(expert_count * per_expert, dtype=jnp.int32)
    marked = jnp.sum(
        (dest_index[None, :, :] == slot_range[:, None, None]).astype(jnp.int32), axis=2
    )
    outgoing = jnp.dot(marked.astype(jnp.bfloat16), tokens, preferred_element_type=jnp.float32)
    outgoing = outgoing.astype(jnp.bfloat16).reshape(expert_count, per_expert, width_local)
    arrived = lax.all_to_all(outgoing, "expert", split_axis=0, concat_axis=0, tiled=True)
    row_data = arrived.reshape(-1, width_local)
    up_local = up_weight[0]
    down_local = down_weight[0]
    before_act = lax.dot_general(
        row_data, up_local, (((1,), (1,)), ((), ())), preferred_element_type=jnp.float32
    )
    share = lax.psum_scatter(before_act, "tensor", scatter_dimension=0, tiled=True)
    hidden = jnp.square(jnp.maximum(share, 0.0)).astype(jnp.bfloat16)
    projected = jnp.dot(
        lax.all_gather(hidden, "tensor", axis=0, tiled=True),
        down_local,
        preferred_element_type=jnp.float32,
    )
    by_block = projected.reshape(expert_count, ctx_count, capacity, width_local)
    totals = lax.psum(by_block, "ctx")
    own_rows = lax.dynamic_index_in_dim(totals, ctx_index, 1, keepdims=False)
    returned = lax.all_to_all(
        own_rows.astype(jnp.bfloat16), "expert", split_axis=0, concat_axis=0, tiled=True
    )
    flattened = returned.reshape(-1, width_local)
    first_row = ctx_index * block_len
    own_ids = lax.dynamic_slice_in_dim(expert_ids, first_row, block_len, 0)
    own_slots = lax.dynamic_slice_in_dim(slot_ids, first_row, block_len, 0)
    own_gates = lax.dynamic_slice_in_dim(route_gates, first_row, block_len, 0)
    row_index = own_ids * capacity + own_slots
    picked = jnp.take(flattened, row_index, axis=0).astype(jnp.float32)
    mixed = jnp.sum(own_gates[:, :, None] * picked, axis=1)
    return mixed.astype(jnp.bfloat16)


def solution(mesh):
    in_specs = (
        P("expert", "tensor"),
        P("expert", None),
        P("expert", None),
        P("expert", "ctx", "tensor"),
        P("expert", "ctx", "tensor"),
    )
    out_specs = P(("expert", "ctx"), "tensor")
    return jax.shard_map(local, mesh=mesh, in_specs=in_specs, out_specs=out_specs, check_vma=False)
```

profile of v0, /device:TPU:0, one launch (start us, length us, event | category | flops | bytes accessed | tf_op | source)
XLA Modules:
  0.0 106.3 jit_solution(8248955880566829928)
XLA Ops:
  6.5 0.0 copy-start
  6.5 0.0 reduce-scatter.2.cloned.1.call-start
  6.5 0.8 copy.26
  7.3 0.1 eq.28
  7.4 0.1 fusion.7
  7.5 0.2 select_reduce_fusion
  7.7 0.1 reshape.38
  7.8 0.1 copy.28
  7.9 0.7 add_add_fusion
  8.6 0.1 convert_reduce_fusion
  8.6 0.0 copy-done
  8.6 0.2 fusion.4
  8.8 8.3 %all_to_all.10 = bf16[4,8,1536]{2,1,0:T(8,128)(2,1)S(1)} all-to-all(bf16[4,8,1536]{2,1,0:T(8,128)(2,1)S(1)} %fusion.4), channel_id=1, replica_groups=mesh['expert'=4,'ctx'=2,'tensor'=4] {'expert'}, dimensions={0} | all-to-all | bytes 196608 | tf_op jit(solution)/shard_map/all_to_all | solution.py:35
  17.2 0.0 copy-start.1
  17.2 12.8 %fusion.2 = f32[32,6144]{1,0:T(8,128)} fusion(bf16[1,6144,1536]{2,1,0:T(8,128)(2,1)} %param.8, bf16[4,8,1536]{2,1,0:T(8,128)(2,1)S(1)} %all_to_all.10), kind=kOutput, calls=%fused_computation.3 | convolution fusion | flops 603979776 | bytes 19759104 | tf_op jit(solution)/shard_map/dot_general | solution.py:39
  30.0 0.0 reduce-scatter.2.cloned.1.call-update
  30.0 0.1 reshape.44
  30.1 23.5 %reduce-scatter.2.cloned.1.call-done = f32[8,6144]{1,0:T(8,128)} async-done(((f32[32,6144]{1,0:T(8,128)}), f32[8,6144]{1,0:T(8,128)}) %reduce-scatter.2.cloned.1.call-update) | async-done | bytes 196624 | tf_op jit(solution)/shard_map/reduce_scatter | solution.py:42
  53.6 0.9 multiply_convert_fusion
  54.6 15.3 %all_gather.3 = bf16[32,6144]{1,0:T(8,128)(2,1)S(1)} all-gather(bf16[8,6144]{1,0:T(8,128)(2,1)S(1)} %multiply_convert_fusion), channel_id=1, replica_groups=mesh['expert'=4,'ctx'=2,'tensor'=4] {'tensor'}, dimensions={0}, use_global_device_ids=true | all-gather | bytes 491520 | tf_op jit(solution)/shard_map/all_gather | solution.py:45
  69.8 0.1 dot_general.13
  70.0 9.6 %fusion = f32[4,2,4,1536]{3,2,1,0:T(4,128)S(1)} fusion(bf16[4,2,4,6144]{3,2,1,0:T(4,128)(2,1)S(1)} %dot_general.13, bf16[1,6144,1536]{2,1,0:T(8,128)(2,1)} %param.9), kind=kOutput, calls=%fused_computation.1 | convolution fusion | flops 603979776 | bytes 19464192 | tf_op jit(solution)/shard_map/dot_general | solution.py:44
  79.6 10.5 %all-reduce.1 = bf16[4,2,4,1536]{3,2,1,0:T(4,128)(2,1)S(1)} all-reduce(f32[4,2,4,1536]{3,2,1,0:T(4,128)S(1)} %fusion), channel_id=1, replica_groups=mesh['expert'=4,'ctx'=2,'tensor'=4] {'ctx'}, use_global_device_ids=true, to_apply=%region_4.5 | all-reduce | flops 49152 | bytes 294912 | tf_op jit(solution)/shard_map/psum | solution.py:50
  90.0 0.6 fusion.6
  90.7 3.3 %all-to-all-start.1 = ((bf16[4,4,1536]{2,1,0:T(4,128)(2,1)}), bf16[4,4,1536]{2,1,0:T(4,128)(2,1)S(1)}, u32[]{:S(2)}, u32[]{:S(2)}) async-start(bf16[4,4,1536]{2,1,0:T(4,128)(2,1)} %fusion.6), calls=%async_computation.2 | async-start | bytes 98304 | tf_op jit(solution)/shard_map/all_to_all | solution.py:52
  93.9 0.0 copy-done.1
  93.9 0.1 constant_dynamic-slice_fusion
  94.0 0.1 copy.25
  94.1 3.8 %all-to-all-done.1 = bf16[4,4,1536]{2,1,0:T(4,128)(2,1)S(1)} async-done(((bf16[4,4,1536]{2,1,0:T(4,128)(2,1)}), bf16[4,4,1536]{2,1,0:T(4,128)(2,1)S(1)}, u32[]{:S(2)}, u32[]{:S(2)}) %all-to-all-start.1) | async-done | bytes 49184 | tf_op jit(solution)/shard_map/all_to_all | solution.py:52
  98.0 0.6 gather_fusion
  98.6 0.8 multiply_reduce_fusion
  (6 shorter events, 0.1 us)
Async XLA Ops:
  6.5 2.1 %copy-start = (bf16[16,1536]{1,0:T(8,128)(2,1)S(1)}, bf16[16,1536]{1,0:T(8,128)(2,1)}, u32[]{:S(2)}) copy-start(bf16[16,1536]{1,0:T(8,128)(2,1)} %param.5) | copy-start | bytes 147460
  6.5 47.1 %reduce-scatter.2.cloned.1.call-start = ((), (), s32[]{:S(2)}) async-start(), calls=%async_computation.3 | async-start | bytes 983040 | tf_op jit(solution)/shard_map/reduce_scatter | solution.py:42
  17.2 76.8 %copy-start.1 = (f32[16,2]{0,1:T(2,128)S(1)}, f32[16,2]{0,1:T(2,128)}, u32[]{:S(2)}) copy-start(f32[16,2]{0,1:T(2,128)} %param.7) | copy-start | bytes 388
  90.7 7.3 %all-to-all-start.1 = ((bf16[4,4,1536]{2,1,0:T(4,128)(2,1)}), bf16[4,4,1536]{2,1,0:T(4,128)(2,1)S(1)}, u32[]{:S(2)}, u32[]{:S(2)}) async-start(bf16[4,4,1536]{2,1,0:T(4,128)(2,1)} %fusion.6), calls=%async_computation.2 | async-start | bytes 98304 | tf_op jit(solution)/shard_map/all_to_all | solution.py:52
Sparse Core Ops, SparseCore 0:
  30.1 23.4 reduce-scatter.1
where the time goes:
time: 107 us; the launch traced here: 106 us
  blocking collectives  34 us (32%)
  waiting for transfers between devices  27.3 us (26%)
  matrix products  22.6 us (21%)
  between operations  13.5 us (13%)
  starting transfers between devices  3.27 us (3%)
  other arithmetic  2.87 us (3%)
  local copies, waits for them, and re-layouts  2.69 us (3%)
    reduce_scatter x1, waiting for transfers between devices, local(): lax.psum_scatter(before_act, 'tensor', scatter_dimension=0, tiled=True)  23.5 us
    all_gather x1, blocking collectives, local(): lax.all_gather(hidden, 'tensor', axis=0, tiled=True)  15.3 us
    dot_general x1, matrix products, local(): lax.dot_general(row_data, up_local, (((1,), (1,)), ((), ())), preferred_e...  12.8 us
    psum x1, blocking collectives, local(): totals = lax.psum(by_block, 'ctx')  10.5 us
    dot_general x1, matrix products, local(): jnp.dot(lax.all_gather(hidden, 'tensor', axis=0, tiled=True), down_local,...  9.55 us
    all_to_all x1, blocking collectives, local(): lax.all_to_all(outgoing, 'expert', split_axis=0, concat_axis=0, tiled=True)  8.33 us
    all_to_all x1, waiting for transfers between devices, local(): lax.all_to_all(own_rows.astype(jnp.bfloat16), 'expert', split_axis=0, con...  3.83 us
    all_to_all x1, starting transfers between devices, local(): lax.all_to_all(own_rows.astype(jnp.bfloat16), 'expert', split_axis=0, con...  3.27 us
  transfers between devices with their start and end apart: 2, of which 2 were waited for; matrix products, arithmetic and copies ran while one was open for 0% of the time, Pallas kernels for 0%

commit v1 on v0

--- a/solution.py
+++ b/solution.py
@@ -47,7 +47,7 @@
         preferred_element_type=jnp.float32,
     )
     by_block = projected.reshape(expert_count, ctx_count, capacity, width_local)
-    totals = lax.psum(by_block, "ctx")
+    totals = jnp.sum(lax.all_gather(by_block, "ctx"), axis=0)
     own_rows = lax.dynamic_index_in_dim(totals, ctx_index, 1, keepdims=False)
     returned = lax.all_to_all(
         own_rows.astype(jnp.bfloat16), "expert", split_axis=0, concat_axis=0, tiled=True

time: 107 us -> 103 us (0.963)
  blocking collectives: 34 us -> 29.9 us
    psum x1 -> x0, blocking collectives: 10.5 us -> none  [local(): totals = lax.psum(by_block, 'ctx')]
    all_gather x0 -> x1, blocking collectives: none -> 6.34 us  [local(): totals = jnp.sum(lax.all_gather(by_block, 'ctx'), axis=0)]
where the time goes in v1:
time: 103 us; the launch traced here: 102 us
  blocking collectives  29.9 us (29%)
  waiting for transfers between devices  27.3 us (27%)
  matrix products  22.6 us (22%)
  between operations  13.5 us (13%)
  starting transfers between devices  3.27 us (3%)
  other arithmetic  2.99 us (3%)
  local copies, waits for them, and re-layouts  2.69 us (3%)
    reduce_scatter x1, waiting for transfers between devices, local(): lax.psum_scatter(before_act, 'tensor', scatter_dimension=0, tiled=True)  23.5 us
    all_gather x1, blocking collectives, local(): lax.all_gather(hidden, 'tensor', axis=0, tiled=True)  15.3 us
    dot_general x1, matrix products, local(): lax.dot_general(row_data, up_local, (((1,), (1,)), ((), ())), preferred_e...  12.8 us
    dot_general x1, matrix products, local(): jnp.dot(lax.all_gather(hidden, 'tensor', axis=0, tiled=True), down_local,...  9.55 us
    all_to_all x1, blocking collectives, local(): lax.all_to_all(outgoing, 'expert', split_axis=0, concat_axis=0, tiled=True)  8.33 us
    all_gather x1, blocking collectives, local(): totals = jnp.sum(lax.all_gather(by_block, 'ctx'), axis=0)  6.34 us
    all_to_all x1, waiting for transfers between devices, local(): lax.all_to_all(own_rows.astype(jnp.bfloat16), 'expert', split_axis=0, con...  3.83 us
    all_to_all x1, starting transfers between devices, local(): lax.all_to_all(own_rows.astype(jnp.bfloat16), 'expert', split_axis=0, con...  3.27 us
  transfers between devices with their start and end apart: 2, of which 2 were waited for; matrix products, arithmetic and copies ran while one was open for 0% of the time, Pallas kernels for 0%

profile of v1, /device:TPU:0, one launch (start us, length us, event | category | flops | bytes accessed | tf_op | source)
XLA Modules:
  0.0 102.3 jit_solution(10982293325440186220)
XLA Ops:
  6.5 0.0 copy-start
  6.5 0.0 reduce-scatter.2.cloned.1.call-start
  6.5 0.8 copy.32
  7.3 0.1 eq.28
  7.4 0.1 fusion.7
  7.5 0.2 select_reduce_fusion
  7.7 0.1 reshape.42
  7.8 0.1 copy.34
  7.9 0.7 add_add_fusion
  8.6 0.1 convert_reduce_fusion
  8.6 0.0 copy-done
  8.6 0.2 fusion.4
  8.8 8.3 %all_to_all.10 = bf16[4,8,1536]{2,1,0:T(8,128)(2,1)S(1)} all-to-all(bf16[4,8,1536]{2,1,0:T(8,128)(2,1)S(1)} %fusion.4), channel_id=1, replica_groups=mesh['expert'=4,'ctx'=2,'tensor'=4] {'expert'}, dimensions={0} | all-to-all | bytes 196608 | tf_op jit(solution)/shard_map/all_to_all | solution.py:35
  17.2 0.0 copy-start.1
  17.2 12.8 %fusion.2 = f32[32,6144]{1,0:T(8,128)} fusion(bf16[1,6144,1536]{2,1,0:T(8,128)(2,1)} %param.8, bf16[4,8,1536]{2,1,0:T(8,128)(2,1)S(1)} %all_to_all.10), kind=kOutput, calls=%fused_computation.3 | convolution fusion | flops 603979776 | bytes 19759104 | tf_op jit(solution)/shard_map/dot_general | solution.py:39
  30.0 0.0 reduce-scatter.2.cloned.1.call-update
  30.0 0.1 reshape.49
  30.1 23.5 %reduce-scatter.2.cloned.1.call-done = f32[8,6144]{1,0:T(8,128)} async-done(((f32[32,6144]{1,0:T(8,128)}), f32[8,6144]{1,0:T(8,128)}) %reduce-scatter.2.cloned.1.call-update) | async-done | bytes 196624 | tf_op jit(solution)/shard_map/reduce_scatter | solution.py:42
  53.6 0.9 multiply_convert_fusion
  54.6 15.3 %all_gather.6 = bf16[32,6144]{1,0:T(8,128)(2,1)S(1)} all-gather(bf16[8,6144]{1,0:T(8,128)(2,1)S(1)} %multiply_convert_fusion), channel_id=1, replica_groups=mesh['expert'=4,'ctx'=2,'tensor'=4] {'tensor'}, dimensions={0}, use_global_device_ids=true | all-gather | bytes 491520 | tf_op jit(solution)/shard_map/all_gather | solution.py:45
  69.8 0.1 reshape.45
  70.0 9.6 %fusion = f32[4,2,4,1536]{3,2,1,0:T(4,128)S(1)} fusion(bf16[4,2,4,6144]{3,2,1,0:T(4,128)(2,1)S(1)} %reshape.45, bf16[1,6144,1536]{2,1,0:T(8,128)(2,1)} %param.9), kind=kOutput, calls=%fused_computation.1 | convolution fusion | flops 603979776 | bytes 19464192 | tf_op jit(solution)/shard_map/dot_general | solution.py:44
  79.6 6.3 %all-gather = f32[8,2,4,1536]{3,2,1,0:T(4,128)S(1)} all-gather(f32[4,2,4,1536]{3,2,1,0:T(4,128)S(1)} %fusion), channel_id=2, replica_groups=mesh['expert'=4,'ctx'=2,'tensor'=4] {'ctx'}, dimensions={0}, use_global_device_ids=true | all-gather | bytes 589824 | tf_op jit(solution)/shard_map/all_gather | solution.py:50
  85.9 0.1 reduce_sum.38
  86.0 0.6 fusion.6
  86.7 3.3 %all-to-all-start.1 = ((bf16[4,4,1536]{2,1,0:T(4,128)(2,1)}), bf16[4,4,1536]{2,1,0:T(4,128)(2,1)S(1)}, u32[]{:S(2)}, u32[]{:S(2)}) async-start(bf16[4,4,1536]{2,1,0:T(4,128)(2,1)} %fusion.6), calls=%async_computation.2 | async-start | bytes 98304 | tf_op jit(solution)/shard_map/all_to_all | solution.py:52
  89.9 0.0 copy-done.1
  89.9 0.1 constant_dynamic-slice_fusion
  90.0 0.1 copy.31
  90.1 3.8 %all-to-all-done.1 = bf16[4,4,1536]{2,1,0:T(4,128)(2,1)S(1)} async-done(((bf16[4,4,1536]{2,1,0:T(4,128)(2,1)}), bf16[4,4,1536]{2,1,0:T(4,128)(2,1)S(1)}, u32[]{:S(2)}, u32[]{:S(2)}) %all-to-all-start.1) | async-done | bytes 49184 | tf_op jit(solution)/shard_map/all_to_all | solution.py:52
  94.0 0.6 gather_fusion
  94.6 0.8 multiply_reduce_fusion
  (6 shorter events, 0.1 us)
Async XLA Ops:
  6.5 2.1 %copy-start = (bf16[16,1536]{1,0:T(8,128)(2,1)S(1)}, bf16[16,1536]{1,0:T(8,128)(2,1)}, u32[]{:S(2)}) copy-start(bf16[16,1536]{1,0:T(8,128)(2,1)} %param.5) | copy-start | bytes 147460
  6.5 47.1 %reduce-scatter.2.cloned.1.call-start = ((), (), s32[]{:S(2)}) async-start(), calls=%async_computation.3 | async-start | bytes 983040 | tf_op jit(solution)/shard_map/reduce_scatter | solution.py:42
  17.2 72.8 %copy-start.1 = (f32[16,2]{0,1:T(2,128)S(1)}, f32[16,2]{0,1:T(2,128)}, u32[]{:S(2)}) copy-start(f32[16,2]{0,1:T(2,128)} %param.7) | copy-start | bytes 388
  86.7 7.3 %all-to-all-start.1 = ((bf16[4,4,1536]{2,1,0:T(4,128)(2,1)}), bf16[4,4,1536]{2,1,0:T(4,128)(2,1)S(1)}, u32[]{:S(2)}, u32[]{:S(2)}) async-start(bf16[4,4,1536]{2,1,0:T(4,128)(2,1)} %fusion.6), calls=%async_computation.2 | async-start | bytes 98304 | tf_op jit(solution)/shard_map/all_to_all | solution.py:52
Sparse Core Ops, SparseCore 0:
  30.1 23.4 reduce-scatter.1
